TPU v7x, 32 devices: a whole 2x2x4 slice. The times are simulated.
32 devices in a mesh: group: 2 (over y), tensor: 4 (over z), dp: 4 (over x, core).
Axes of the slice: x: 2, y: 2, z: 4, core: 2. Of those that a mesh axis runs over, the one named last changes fastest.
Arguments:
- teacher_input: bfloat16 [16, 257, 6144], P(('group', 'dp')), parts along dimension 0, may hold values from -1000 to 1000
- teacher_gain: float32 [6144], replicated, may hold values from 0.5 to 2
- teacher_weight: bfloat16 [6144, 2, 6144], P('dp', None, 'tensor'), may hold values from -30 to 30
- head_counts: int32 [48, 16], replicated, may hold values from 0 to 3
- assignment: int32 [16], P(('group', 'dp')), parts along dimension 0, may hold values from 0 to 7, each once
- student_input: bfloat16 [16, 257, 1024], P(('group', 'dp')), parts along dimension 0, may hold values from -1000 to 1000
- student_gain: float32 [1024], replicated, may hold values from 0.5 to 2
- student_bias: float32 [1024], replicated, may hold values from -3 to 3
- student_weight: bfloat16 [1024, 2048], P(None, 'tensor'), may hold values from -30 to 30
Outputs:
- weight_grad: float32 [2048, 2048], P('group', 'tensor'), parts along dimension 0
There are 2 independent parts, one for each index of `group`. A program takes and returns all parts, laid end to end along the dimension named above; an argument that names none is the same for every part. Nothing has to cross between parts.
Inputs may be any that keep to these rules, and one draw needn't show every extreme that they name: `assignment`: every image index of the group appears exactly once.
All inputs are finite; a program needn't handle non-finite values.
Results may differ from a plain program's by a relative error of at most 0.013.
The roundings to bfloat16 on the way count: a program that leaves them out, or rounds other values in their place, can miss the bound.
Values may be sent and summed in bfloat16 or wider, within the bound.
A program may use at most 192 MiB of HBM per device.

v0:
```python
import jax
import jax.numpy as jnp
from jax import lax
from jax.sharding import PartitionSpec as P

HD_T = 128
D_S = 1024
HD_S = 64
QROWS = 128
DIVISOR = 72


def layer_norm(values, gain, shift):
    wide = values.astype(jnp.float32)
    center = wide - jnp.mean(wide, axis=-1, keepdims=True)
    spread = jnp.mean(center * center, axis=-1, keepdims=True)
    return center * lax.rsqrt(spread + 1e-06) * gain + shift


def on_device(
    teacher_input,
    teacher_gain,
    teacher_weight,
    head_counts,
    assignment,
    student_input,
    student_gain,
    student_bias,
    student_weight,
):
    images = teacher_input.shape[0]
    tokens = teacher_input.shape[1]
    width_t = teacher_input.shape[2]
    teacher_cols = teacher_weight.shape[2]
    heads_here = teacher_cols // HD_T
    student_heads = student_weight.shape[1] // (2 * HD_S)
    tensor_place = lax.axis_index("tensor")
    teacher_normed = layer_norm(teacher_input, teacher_gain, 0.0).astype(jnp.bfloat16)
    normed_query = teacher_normed[:, :QROWS].reshape(images * QROWS, width_t)
    normed_keys = teacher_normed.reshape(images * tokens, width_t)
    piece = lax.all_gather(teacher_weight, "dp", axis=0, tiled=True)
    new_query = jnp.dot(normed_query, piece[:, 0, :], preferred_element_type=jnp.float32)
    new_keys = jnp.dot(normed_keys, piece[:, 1, :], preferred_element_type=jnp.float32)
    teacher_query = (
        (new_query * HD_T ** (-0.5)).astype(jnp.bfloat16).reshape(images, QROWS, heads_here, HD_T)
    )
    teacher_keys = new_keys.astype(jnp.bfloat16).reshape(images, tokens, heads_here, HD_T)
    teacher_scores = jnp.einsum(
        "bqhd,bkhd->bhqk", teacher_query, teacher_keys, preferred_element_type=jnp.float32
    )
    teacher_maps = jax.nn.softmax(teacher_scores, axis=-1).astype(jnp.bfloat16)
    own_counts = lax.dynamic_slice_in_dim(
        head_counts, tensor_place * heads_here, heads_here, 0
    ).astype(jnp.bfloat16)
    folded = lax.psum_scatter(
        (
            jnp.einsum(
                "bgqk,gs->sbqk", teacher_maps, own_counts, preferred_element_type=jnp.float32
            )
            / DIVISOR
        ).astype(jnp.bfloat16),
        "tensor",
        scatter_dimension=0,
        tiled=True,
    )
    piece = lax.all_gather(folded, "dp", axis=1, tiled=True)
    width_piece = piece.shape[1]
    positions = jnp.arange(width_piece, dtype=jnp.int32)
    picker = (assignment[:, None] == positions[None, :]).astype(jnp.bfloat16)
    target = jnp.einsum("ji,hiqk->hjqk", picker, piece, preferred_element_type=jnp.float32).astype(
        jnp.bfloat16
    )
    student_normed = layer_norm(student_input, student_gain, student_bias).astype(jnp.bfloat16)
    normed_front = student_normed[:, :QROWS]
    packed = student_weight.reshape(D_S, student_heads, 2, HD_S)
    weight_query = packed[:, :, 0, :].reshape(D_S, student_heads * HD_S)
    weight_key = packed[:, :, 1, :].reshape(D_S, student_heads * HD_S)
    student_query = (
        jnp.einsum("btd,dc->btc", normed_front, weight_query, preferred_element_type=jnp.float32)
        * HD_S ** (-0.5)
    ).astype(jnp.bfloat16)
    student_keys = jnp.einsum(
        "btd,dc->btc", student_normed, weight_key, preferred_element_type=jnp.float32
    ).astype(jnp.bfloat16)
    split_query = student_query.reshape(images, QROWS, student_heads, HD_S)
    split_keys = student_keys.reshape(images, tokens, student_heads, HD_S)
    probs = jax.nn.softmax(
        jnp.einsum("bqhd,bkhd->hbqk", split_query, split_keys, preferred_element_type=jnp.float32),
        axis=-1,
    )
    target_wide = target.astype(jnp.float32)
    score_grad = (probs * jnp.sum(target_wide, axis=-1, keepdims=True) - target_wide).astype(
        jnp.bfloat16
    )
    query_grad = (
        jnp.einsum("hbqk,bkhd->bqhd", score_grad, split_keys, preferred_element_type=jnp.float32)
        * HD_S ** (-0.5)
    ).astype(jnp.bfloat16)
    key_grad = jnp.einsum(
        "hbqk,bqhd->bkhd", score_grad, split_query, preferred_element_type=jnp.float32
    ).astype(jnp.bfloat16)
    grad_query = jnp.einsum(
        "fkm,fkp->mp",
        normed_front,
        query_grad.reshape(images, QROWS, student_heads * HD_S),
        preferred_element_type=jnp.float32,
    )
    grad_key = jnp.einsum(
        "oip,ois->ps",
        student_normed,
        key_grad.reshape(images, tokens, student_heads * HD_S),
        preferred_element_type=jnp.float32,
    )
    local_grad = jnp.stack(
        [grad_query.reshape(D_S, student_heads, HD_S), grad_key.reshape(D_S, student_heads, HD_S)],
        axis=2,
    )
    local_grad = local_grad.reshape(D_S, student_heads * 2 * HD_S)
    return lax.psum(local_grad.astype(jnp.bfloat16), "dp").astype(jnp.float32)


def solution(mesh):
    placed = (
        P(("group", "dp"), None, None),
        P(),
        P("dp", None, "tensor"),
        P(),
        P(("group", "dp")),
        P(("group", "dp"), None, None),
        P(),
        P(),
        P(None, "tensor"),
    )
    return jax.shard_map(
        on_device, mesh=mesh, in_specs=placed, out_specs=P("group", "tensor"), check_vma=False
    )
```

profile of v0, /device:TPU:0, one launch (start us, length us, event | category | flops | bytes accessed | tf_op | source)
XLA Modules:
  0.0 448.8 jit_solution(8952922629155033750)
XLA Ops:
  6.5 8.8 %copy.104 = bf16[1536,2,1536]{2,0,1:T(8,128)(2,1)} copy(bf16[1536,2,1536]{2,1,0:T(2,128)(2,1)} %param.11) | data formatting | bytes 18874368 | tf_op args[2]
  15.4 6.3 %convert_reduce_fusion = f32[2,257]{1,0:T(2,128)S(1)} fusion(bf16[2,257,6144]{2,0,1:T(2,128)(2,1)} %param.9), kind=kLoop, calls=%fused_computation.6 | loop fusion | flops 6315518 | bytes 6318088 | tf_op jit(solution)/shard_map/reduce_sum | solution.py:15
  21.7 3.5 fusion.5
  25.2 4.1 fusion.7
  29.4 4.6 %copy-done.1 = bf16[2,257,6144]{2,1,0:T(8,128)(2,1)} copy-done((bf16[2,257,6144]{2,1,0:T(8,128)(2,1)}, bf16[2,257,6144]{2,1,0:T(8,128)(2,1)S(1)}, u32[]{:S(2)}) %copy-start.1) | copy-done | bytes 6316056
  34.0 9.8 %reshape.81 = bf16[514,6144]{1,0:T(8,128)(2,1)} reshape(bf16[2,257,6144]{2,1,0:T(8,128)(2,1)} %copy-done.1) | data formatting | bytes 12632064 | tf_op jit(solution)/shard_map/reshape | solution.py:40
  43.7 202.4 %all-gather.3.cloned.1.call-done = bf16[6144,2,1536]{2,0,1:T(8,128)(2,1)} async-done(((bf16[1536,2,1536]{2,0,1:T(8,128)(2,1)}), bf16[6144,2,1536]{2,0,1:T(8,128)(2,1)}) %all-gather.3.cloned.1.call-update) | async-done | bytes 37748752 | tf_op jit(solution)/shard_map/all_gather | solution.py:41
  246.1 10.2 %fusion.10 = bf16[256,1536]{1,0:T(8,128)(2,1)} fusion(bf16[256,6144]{1,0:T(8,128)(2,1)S(1)} %bitcast.99, bf16[6144,2,1536]{2,0,1:T(8,128)(2,1)} %all-gather.3.cloned.1.call-done), kind=kOutput, calls=%fused_computation.19 | convolution fusion | flops 4832624640 | bytes 22806528 | tf_op jit(solution)/shard_map/dot_general | solution.py:42
  256.3 2.4 reshape.95
  258.6 16.2 %fusion.8 = bf16[514,1536]{1,0:T(8,128)(2,1)S(1)} fusion(bf16[514,6144]{1,0:T(8,128)(2,1)} %reshape.81, bf16[6144,2,1536]{2,0,1:T(8,128)(2,1)} %all-gather.3.cloned.1.call-done), kind=kOutput, calls=%fused_computation.15 | convolution fusion | flops 9702214656 | bytes 26843136 | tf_op jit(solution)/shard_map/dot_general | solution.py:43
  274.8 2.4 reshape.82
  277.2 3.1 fusion.61
  281.8 2.9 copy.109
  286.1 85.7 %all-reduce.6.cloned.1.call-done = bf16[16,2,128,257]{2,1,3,0:T(2,128)(2,1)} async-done(((bf16[16,2,128,257]{2,1,3,0:T(2,128)(2,1)}), bf16[16,2,128,257]{2,1,3,0:T(2,128)(2,1)}) %all-reduce.6.cloned.1.call-update) | async-done | bytes 2105360
  371.8 1.4 constant_dynamic-slice_fusion
  373.2 1.0 copy.110
  377.6 1.0 copy-done.3
  380.1 16.0 %all-gather.5.cloned.1.call-done = bf16[4,8,128,257]{2,0,3,1:T(4,128)(2,1)} async-done(((bf16[4,2,128,257]{2,0,3,1:T(4,128)(2,1)}), bf16[4,8,128,257]{2,0,3,1:T(4,128)(2,1)}) %all-gather.5.cloned.1.call-update) | async-done | bytes 2105360 | tf_op jit(solution)/shard_map/all_gather | solution.py:66
  396.1 2.4 fusion.17
  399.4 1.5 fusion.24
  401.0 1.0 fusion.25
  402.1 1.1 copy.117
  403.2 36.5 %all-reduce.4.cloned.1.call-done = bf16[1024,512]{0,1:T(8,128)(2,1)} async-done(((bf16[1024,512]{0,1:T(8,128)(2,1)}), bf16[1024,512]{0,1:T(8,128)(2,1)}) %all-reduce.4.cloned.1.call-update) | async-done | bytes 1048592 | tf_op jit(solution)/shard_map/psum | solution.py:119
  439.7 2.6 copy.118
  (52 shorter events, 8.1 us)
Async XLA Ops:
  6.5 239.5 %all-gather.3.cloned.1.call-start = ((), (), s32[]{:S(2)}) async-start(), calls=%async_computation | async-start | bytes 47185920 | tf_op jit(solution)/shard_map/all_gather | solution.py:41
  15.3 356.5 %all-reduce.6.cloned.1.call-start = ((), (), s32[]{:S(2)}) async-start(), calls=%async_computation.3 | async-start | bytes 4210688
  15.4 6.3 %copy-start = (bf16[2,257,6144]{2,0,1:T(2,128)(2,1)S(1)}, bf16[2,257,6144]{2,0,1:T(2,128)(2,1)}, u32[]{:S(2)}) copy-start(bf16[2,257,6144]{2,0,1:T(2,128)(2,1)} %param.9) | copy-start | bytes 18948100
  21.7 3.5 copy-start.5
  29.4 4.6 %copy-start.1 = (bf16[2,257,6144]{2,1,0:T(8,128)(2,1)}, bf16[2,257,6144]{2,1,0:T(8,128)(2,1)S(1)}, u32[]{:S(2)}) copy-start(bf16[2,257,6144]{2,1,0:T(8,128)(2,1)S(1)} %fusion.7) | copy-start | bytes 18948100
  34.0 212.1 %slice-start = ((bf16[2,257,6144]{2,1,0:T(8,128)(2,1)}), bf16[2,128,6144]{2,1,0:T(8,128)(2,1)S(1)}, s32[]{:S(2)}) async-start(bf16[2,257,6144]{2,1,0:T(8,128)(2,1)} %copy-done.1), calls=%async_computation.4 | async-start | bytes 6291456 | tf_op jit(solution)/shard_map/slice | solution.py:39
  280.4 0.7 copy-start.6
  281.8 3.0 copy-start.10
  284.8 89.5 %copy-start.4 = (bf16[1024,512]{1,0:T(8,128)(2,1)S(1)}, bf16[1024,512]{1,0:T(8,128)(2,1)}, u32[]{:S(2)}) copy-start(bf16[1024,512]{1,0:T(8,128)(2,1)} %param.17) | copy-start | bytes 3145732
  284.8 111.3 %all-gather.5.cloned.1.call-start = ((), (), s32[]{:S(2)}) async-start(), calls=%async_computation.1 | async-start | bytes 2631680 | tf_op jit(solution)/shard_map/all_gather | solution.py:66
  286.1 89.0 %copy-start.2 = (bf16[2,257,1024]{2,0,1:T(2,128)(2,1)S(1)}, bf16[2,257,1024]{2,0,1:T(2,128)(2,1)}, u32[]{:S(2)}) copy-start(bf16[2,257,1024]{2,0,1:T(2,128)(2,1)} %param.14) | copy-start | bytes 3158020
  374.3 65.4 %all-reduce.4.cloned.1.call-start = ((), (), s32[]{:S(2)}) async-start(), calls=%async_computation.2 | async-start | bytes 2097152 | tf_op jit(solution)/shard_map/psum | solution.py:119
  375.1 0.9 copy-start.7
  375.1 0.9 copy-start.8
  377.6 1.0 copy-start.3
  378.6 17.5 %copy-start.9 = (s32[2]{0:T(128)S(1)}, s32[2]{0:T(128)}, u32[]{:S(2)}) copy-start(s32[2]{0:T(128)} %param.13) | copy-start | bytes 28
Sparse Core Ops, SparseCore 0:
  15.5 230.5 all-gather.2
  284.9 86.8 all-reduce.5
  374.4 21.6 all-gather.4
  403.3 36.2 all-reduce.3
where the time goes:
time: 449 us
  waiting for transfers between devices  341 us (76%)
  local copies, waits for them, and re-layouts  40.2 us (9%)
  matrix products  36.8 us (8%)
  other arithmetic  17.1 us (4%)
  between operations  14 us (3%)
    all_gather x1, waiting for transfers between devices, on_device(): piece = lax.all_gather(teacher_weight, 'dp', axis=0, tiled=True)  202 us
    unnamed x5, waiting for transfers between devices  85.8 us
    psum x1, waiting for transfers between devices, on_device(): return lax.psum(local_grad.astype(jnp.bfloat16), 'dp').astype(jnp.float32)  36.5 us
    unnamed x26, local copies, waits for them, and re-layouts  17.6 us
    dot_general x1, matrix products, on_device(): jnp.dot(normed_keys, piece[:, 1, :], preferred_element_type=jnp.float32)  16.2 us
    all_gather x1, waiting for transfers between devices, on_device(): piece = lax.all_gather(folded, 'dp', axis=1, tiled=True)  16 us
    dot_general x1, matrix products, on_device(): jnp.dot(normed_query, piece[:, 0, :], preferred_element_type=jnp.float32)  10.2 us
    reshape x1, local copies, waits for them, and re-layouts, on_device(): normed_keys = teacher_normed.reshape(images * tokens, width_t)  9.77 us
  transfers between devices with their start and end apart: 4, of which 4 were waited for; matrix products, arithmetic and copies ran while one was open for 6% of the time, Pallas kernels for 0%

commit v1 on v0

--- a/solution.py
+++ b/solution.py
@@ -38,7 +38,14 @@
     teacher_normed = layer_norm(teacher_input, teacher_gain, 0.0).astype(jnp.bfloat16)
     normed_query = teacher_normed[:, :QROWS].reshape(images * QROWS, width_t)
     normed_keys = teacher_normed.reshape(images * tokens, width_t)
-    piece = lax.all_gather(teacher_weight, "dp", axis=0, tiled=True)
+    size = lax.axis_size("dp")
+    hops = [(i, (i + 1) % size) for i in range(size)]
+    pieces = [teacher_weight]
+    for far in range(1, size):
+        pieces = [lax.ppermute(pieces[0], "dp", hops), *pieces]
+    whole = jnp.concatenate(pieces, axis=0)
+    offset = (lax.axis_index("dp") + 1) * pieces[-1].shape[0]
+    piece = jnp.roll(whole, offset, axis=0)
     new_query = jnp.dot(normed_query, piece[:, 0, :], preferred_element_type=jnp.float32)
     new_keys = jnp.dot(normed_keys, piece[:, 1, :], preferred_element_type=jnp.float32)
     teacher_query = (

time: 449 us -> 610 us (1.36); the launches traced: 449 us -> 603 us
  waiting for transfers between devices: 341 us -> 430 us
  local copies, waits for them, and re-layouts: 40.2 us -> 104 us
    ppermute x0 -> x3, waiting for transfers between devices: none -> 289 us  [on_device(): pieces = [lax.ppermute(pieces[0], 'dp', hops), *pieces]]
    all_gather x1 -> x0, waiting for transfers between devices: 202 us -> none  [on_device(): piece = lax.all_gather(teacher_weight, 'dp', axis=0, tiled=True)]
    unnamed x26 -> x35, local copies, waits for them, and re-layouts: 17.6 us -> 75.4 us
    concatenate x0 -> x1, local copies, waits for them, and re-layouts: none -> 8.82 us  [on_device(): piece = jnp.roll(whole, offset, axis=0)]
    unnamed x5 -> x4, waiting for transfers between devices: 85.8 us -> 88 us
  transfers between devices with their start and end apart: 4 -> 6, of which waited for: 4 -> 6; matrix products, arithmetic and copies ran while one was open for 6% -> 4% of each run, Pallas kernels for 0% -> 0%
where the time goes in v1:
time: 610 us; the launch traced here: 603 us
  waiting for transfers between devices  430 us (70%)
  local copies, waits for them, and re-layouts  104 us (17%)
  matrix products  37 us (6%)
  other arithmetic  17.2 us (3%)
  between operations  14.3 us (2%)
    ppermute x3, waiting for transfers between devices, on_device(): pieces = [lax.ppermute(pieces[0], 'dp', hops), *pieces]  289 us
    unnamed x4, waiting for transfers between devices  88 us
    unnamed x35, local copies, waits for them, and re-layouts  75.4 us
    psum x1, waiting for transfers between devices, on_device(): return lax.psum(local_grad.astype(jnp.bfloat16), 'dp').astype(jnp.float32)  36.5 us
    all_gather x1, waiting for transfers between devices, on_device(): piece = lax.all_gather(folded, 'dp', axis=1, tiled=True)  16 us
    dot_general x1, matrix products, on_device(): jnp.dot(normed_keys, piece[:, 1, :], preferred_element_type=jnp.float32)  16 us
  transfers between devices with their start and end apart: 6, of which 6 were waited for; matrix products, arithmetic and copies ran while one was open for 4% of the time, Pallas kernels for 0%

profile of v1, /device:TPU:0, one launch (start us, length us, event | category | flops | bytes accessed | tf_op | source)
XLA Modules:
  0.0 602.8 jit_solution(256224490272378922)
XLA Ops:
  6.5 8.8 %copy.110 = bf16[1536,2,1536]{2,0,1:T(8,128)(2,1)} copy(bf16[1536,2,1536]{2,1,0:T(2,128)(2,1)} %param.11) | data formatting | bytes 18874368 | tf_op args[2]
  15.8 104.5 %collective-permute-done = bf16[1536,2,1536]{2,0,1:T(8,128)(2,1)S(1)} collective-permute-done((bf16[1536,2,1536]{2,0,1:T(8,128)(2,1)}, bf16[1536,2,1536]{2,0,1:T(8,128)(2,1)S(1)}, u32[]{:S(2)}, u32[]{:S(2)}) %collective-permute-start) | collective-permute-done | bytes 9437216 | tf_op jit(solution)/shard_map/ppermute | solution.py:45
  120.3 3.7 copy-done.2
  124.0 104.2 %collective-permute-done.1 = bf16[1536,2,1536]{2,0,1:T(8,128)(2,1)} collective-permute-done((bf16[1536,2,1536]{2,0,1:T(8,128)(2,1)S(1)}, bf16[1536,2,1536]{2,0,1:T(8,128)(2,1)}, u32[]{:S(2)}, u32[]{:S(2)}) %collective-permute-start.1) | collective-permute-done | bytes 9437216 | tf_op jit(solution)/shard_map/ppermute | solution.py:45
  228.2 6.3 %convert_reduce_fusion = f32[2,257]{1,0:T(2,128)S(1)} fusion(bf16[2,257,6144]{2,0,1:T(2,128)(2,1)} %param.9), kind=kLoop, calls=%fused_computation.6 | loop fusion | flops 6315518 | bytes 6318088 | tf_op jit(solution)/shard_map/reduce_sum | solution.py:15
  234.5 3.5 fusion.5
  238.0 4.2 fusion.7
  245.0 6.9 %reshape.81 = bf16[514,6144]{1,0:T(8,128)(2,1)} reshape(bf16[2,257,6144]{2,1,0:T(8,128)(2,1)} %copy-done.1) | data formatting | bytes 12632064 | tf_op jit(solution)/shard_map/reshape | solution.py:40
  251.9 80.7 %collective-permute-done.2 = bf16[1536,2,1536]{2,0,1:T(8,128)(2,1)} collective-permute-done((bf16[1536,2,1536]{2,0,1:T(8,128)(2,1)}, bf16[1536,2,1536]{2,0,1:T(8,128)(2,1)}, u32[]{:S(2)}, u32[]{:S(2)}) %collective-permute-start.2) | collective-permute-done | bytes 9437216 | tf_op jit(solution)/shard_map/ppermute | solution.py:45
  332.6 7.8 %constant_dynamic-update-slice_fusion.7 = bf16[12288,2,1536]{2,0,1:T(8,128)(2,1)} fusion(bf16[1536,2,1536]{2,0,1:T(8,128)(2,1)} %collective-permute-done.2), kind=kLoop, calls=%fused_computation.71 | loop fusion | bytes 18874368
  340.5 7.9 %constant_dynamic-update-slice_fusion.6 = bf16[12288,2,1536]{2,0,1:T(8,128)(2,1)} fusion(bf16[12288,2,1536]{2,0,1:T(8,128)(2,1)} %constant_dynamic-update-slice_fusion.7, bf16[1536,2,1536]{2,0,1:T(8,128)(2,1)} %collective-permute-done.1), kind=kLoop, calls=%fused_computation.70 | loop fusion | bytes 18874368
  348.4 7.9 %constant_dynamic-update-slice_fusion.5 = bf16[12288,2,1536]{2,0,1:T(8,128)(2,1)} fusion(bf16[12288,2,1536]{2,0,1:T(8,128)(2,1)} %constant_dynamic-update-slice_fusion.6, bf16[1536,2,1536]{2,0,1:T(8,128)(2,1)} %copy-done.2), kind=kLoop, calls=%fused_computation.69 | loop fusion | bytes 18874368
  356.3 8.7 %constant_dynamic-update-slice_fusion.4 = bf16[12288,2,1536]{2,0,1:T(8,128)(2,1)} fusion(bf16[12288,2,1536]{2,0,1:T(8,128)(2,1)} %constant_dynamic-update-slice_fusion.5, bf16[1536,2,1536]{2,1,0:T(2,128)(2,1)} %param.11), kind=kLoop, calls=%fused_computation.68 | loop fusion | bytes 18874368
  365.0 7.8 %constant_dynamic-update-slice_fusion.3 = bf16[12288,2,1536]{2,0,1:T(8,128)(2,1)} fusion(bf16[12288,2,1536]{2,0,1:T(8,128)(2,1)} %constant_dynamic-update-slice_fusion.4, bf16[1536,2,1536]{2,0,1:T(8,128)(2,1)} %collective-permute-done.2), kind=kLoop, calls=%fused_computation.67 | loop fusion | bytes 18874368
  372.9 7.9 %constant_dynamic-update-slice_fusion.2 = bf16[12288,2,1536]{2,0,1:T(8,128)(2,1)} fusion(bf16[12288,2,1536]{2,0,1:T(8,128)(2,1)} %constant_dynamic-update-slice_fusion.3, bf16[1536,2,1536]{2,0,1:T(8,128)(2,1)} %collective-permute-done.1), kind=kLoop, calls=%fused_computation.66 | loop fusion | bytes 18874368
  380.8 7.8 %constant_dynamic-update-slice_fusion.1 = bf16[12288,2,1536]{2,0,1:T(8,128)(2,1)} fusion(bf16[12288,2,1536]{2,0,1:T(8,128)(2,1)} %constant_dynamic-update-slice_fusion.2, bf16[1536,2,1536]{2,0,1:T(8,128)(2,1)} %copy-done.2), kind=kLoop, calls=%fused_computation.65 | loop fusion | bytes 18874368
  388.6 8.8 %constant_dynamic-update-slice_fusion = bf16[12288,2,1536]{2,0,1:T(8,128)(2,1)} fusion(bf16[12288,2,1536]{2,0,1:T(8,128)(2,1)} %constant_dynamic-update-slice_fusion.1, bf16[1536,2,1536]{2,1,0:T(2,128)(2,1)} %param.11), kind=kLoop, calls=%fused_computation.64 | loop fusion | bytes 18874368 | tf_op jit(solution)/shard_map/jit(_roll_dynamic)/concatenate | solution.py:48
  397.4 10.6 %fusion.10 = bf16[256,1536]{1,0:T(8,128)(2,1)} fusion(bf16[256,6144]{1,0:T(8,128)(2,1)S(1)} %bitcast.99, bf16[12288,2,1536]{2,0,1:T(8,128)(2,1)} %constant_dynamic-update-slice_fusion, s32[]{:T(128)S(6)} %select_n.18), kind=kOutput, calls=%fused_computation.19 | convolution fusion | flops 4832624640 | bytes 22806532 | tf_op jit(solution)/shard_map/dot_general | solution.py:49
  410.4 16.0 %fusion.8 = bf16[514,1536]{1,0:T(8,128)(2,1)S(1)} fusion(bf16[514,6144]{1,0:T(8,128)(2,1)} %reshape.81, bf16[12288,2,1536]{2,0,1:T(8,128)(2,1)} %constant_dynamic-update-slice_fusion, s32[]{:T(128)S(6)} %select_n.18, s32[]{:T(128)S(6)} %add.54), kind=kOutput, calls=%fused_computation.15 | convolution fusion | flops 9702214656 | bytes 26843144 | tf_op jit(solution)/shard_map/dot_general | solution.py:50
  428.9 3.1 fusion.63
  433.5 2.9 copy.117
  437.7 87.9 %all-reduce.6.cloned.1.call-done = bf16[16,2,128,257]{2,1,3,0:T(2,128)(2,1)} async-done(((bf16[16,2,128,257]{2,1,3,0:T(2,128)(2,1)}), bf16[16,2,128,257]{2,1,3,0:T(2,128)(2,1)}) %all-reduce.6.cloned.1.call-update) | async-done | bytes 2105360
  533.8 16.0 %all-gather.2.cloned.1.call-done = bf16[4,8,128,257]{2,0,3,1:T(4,128)(2,1)} async-done(((bf16[4,2,128,257]{2,0,3,1:T(4,128)(2,1)}), bf16[4,8,128,257]{2,0,3,1:T(4,128)(2,1)}) %all-gather.2.cloned.1.call-update) | async-done | bytes 2105360 | tf_op jit(solution)/shard_map/all_gather | solution.py:73
  557.0 36.5 %all-reduce.4.cloned.1.call-done = bf16[1024,512]{0,1:T(8,128)(2,1)} async-done(((bf16[1024,512]{0,1:T(8,128)(2,1)}), bf16[1024,512]{0,1:T(8,128)(2,1)}) %all-reduce.4.cloned.1.call-update) | async-done | bytes 1048592 | tf_op jit(solution)/shard_map/psum | solution.py:126
  (65 shorter events, 27.9 us)
Async XLA Ops:
  6.5 519.1 %all-reduce.6.cloned.1.call-start = ((), (), s32[]{:S(2)}) async-start(), calls=%async_computation.2 | async-start | bytes 4210688
  15.3 105.0 %collective-permute-start = (bf16[1536,2,1536]{2,0,1:T(8,128)(2,1)}, bf16[1536,2,1536]{2,0,1:T(8,128)(2,1)S(1)}, u32[]{:S(2)}, u32[]{:S(2)}) collective-permute-start(bf16[1536,2,1536]{2,0,1:T(8,128)(2,1)} %copy.110), channel_id=1, source_target_pairs={{0,1},{1,2},{2,3},{3,0},{4,5},{5,6},{6,7},{7,4},{8,9},{9,10},{10,1... | collective-permute-start | bytes 28311560 | tf_op jit(solution)/shard_map/ppermute | solution.py:45
  120.3 3.7 copy-start.2
  124.0 104.2 %collective-permute-start.1 = (bf16[1536,2,1536]{2,0,1:T(8,128)(2,1)S(1)}, bf16[1536,2,1536]{2,0,1:T(8,128)(2,1)}, u32[]{:S(2)}, u32[]{:S(2)}) collective-permute-start(bf16[1536,2,1536]{2,0,1:T(8,128)(2,1)S(1)} %collective-permute-done), channel_id=1, source_target_pairs={{0,1},{1,2},{2,3},{3,0},{4,5},{5,6},{6,7},{7,4},{8,9},{9,10},{10,1... | collective-permute-start | bytes 28311560 | tf_op jit(solution)/shard_map/ppermute | solution.py:45
  228.2 104.4 %collective-permute-start.2 = (bf16[1536,2,1536]{2,0,1:T(8,128)(2,1)}, bf16[1536,2,1536]{2,0,1:T(8,128)(2,1)}, u32[]{:S(2)}, u32[]{:S(2)}) collective-permute-start(bf16[1536,2,1536]{2,0,1:T(8,128)(2,1)} %collective-permute-done.1), channel_id=1, source_target_pairs={{0,1},{1,2},{2,3},{3,0},{4,5},{5,6},{6,7},{7,4},{8,9},{9,10},{10,1... | collective-permute-start | bytes 28311560 | tf_op jit(solution)/shard_map/ppermute | solution.py:45
  228.2 6.3 %copy-start = (bf16[2,257,6144]{2,0,1:T(2,128)(2,1)S(1)}, bf16[2,257,6144]{2,0,1:T(2,128)(2,1)}, u32[]{:S(2)}) copy-start(bf16[2,257,6144]{2,0,1:T(2,128)(2,1)} %param.9) | copy-start | bytes 18948100
  234.5 3.5 copy-start.6
  242.3 2.7 copy-start.1
  388.6 8.8 %slice-start = ((bf16[2,257,6144]{2,1,0:T(8,128)(2,1)}), bf16[2,128,6144]{2,1,0:T(8,128)(2,1)S(1)}, s32[]{:S(2)}) async-start(bf16[2,257,6144]{2,1,0:T(8,128)(2,1)} %copy-done.1), calls=%async_computation.3 | async-start | bytes 6291456 | tf_op jit(solution)/shard_map/slice | solution.py:39
  432.0 0.7 copy-start.7
  433.4 3.0 copy-start.11
  436.4 91.7 %copy-start.5 = (bf16[1024,512]{1,0:T(8,128)(2,1)S(1)}, bf16[1024,512]{1,0:T(8,128)(2,1)}, u32[]{:S(2)}) copy-start(bf16[1024,512]{1,0:T(8,128)(2,1)} %param.17) | copy-start | bytes 3145732
  436.4 113.4 %all-gather.2.cloned.1.call-start = ((), (), s32[]{:S(2)}) async-start(), calls=%async_computation | async-start | bytes 2631680 | tf_op jit(solution)/shard_map/all_gather | solution.py:73
  437.7 91.2 %copy-start.3 = (bf16[2,257,1024]{2,0,1:T(2,128)(2,1)S(1)}, bf16[2,257,1024]{2,0,1:T(2,128)(2,1)}, u32[]{:S(2)}) copy-start(bf16[2,257,1024]{2,0,1:T(2,128)(2,1)} %param.14) | copy-start | bytes 3158020
  528.1 65.4 %all-reduce.4.cloned.1.call-start = ((), (), s32[]{:S(2)}) async-start(), calls=%async_computation.1 | async-start | bytes 2097152 | tf_op jit(solution)/shard_map/psum | solution.py:126
  528.9 0.9 copy-start.8
  528.9 0.9 copy-start.9
  530.3 1.0 copy-start.4
  532.6 17.3 %copy-start.10 = (s32[2]{0:T(128)S(1)}, s32[2]{0:T(128)}, u32[]{:S(2)}) copy-start(s32[2]{0:T(128)} %param.13) | copy-start | bytes 28
Sparse Core Ops, SparseCore 0:
  436.5 89.0 all-reduce.5
  528.2 21.6 all-gather.1
  557.1 36.2 all-reduce.3
